TPU v7x, 512 devices: a whole 4x8x8 slice. The times are simulated.
512 devices in a mesh: panel: 8 (over x, core), sc: 64 (over z, y).
Axes of the slice: x: 4, y: 8, z: 8, core: 2. Of those that a mesh axis runs over, the one named last changes fastest.
Arguments:
- channel: bfloat16 [2, 2048, 1024, 128], P(None, 'sc', 'panel'), may hold values from -0.1875 to 0.1875
- received: bfloat16 [2, 2048, 1024], P(None, 'sc', 'panel'), may hold values from -6 to 6
- noise: float32 [2048], P('sc'), may hold values from 0.05 to 0.5
- steps: float32 [3, 2, 128, 128], replicated, may hold values from -0.5 to 0.5
- cotangent: float32 [2, 2048, 128], P(None, 'sc', 'panel'), may hold values from -6 to 6
- counts: int32 [64], P('sc'), may hold values from 1 to 32, 1280 in all
Outputs:
- grad_channel: bfloat16 [2, 2048, 1024, 128], P(None, 'sc', 'panel')
- grad_received: bfloat16 [2, 2048, 1024], P(None, 'sc', 'panel')
- grad_steps: float32 [3, 2, 128, 128], replicated
Inputs may be any that keep to these rules, and one draw needn't show every extreme that they name: `counts`: each block has between 1 and 32 rostered subcarriers, and some block has all 32.
All inputs are finite; a program needn't handle non-finite values.
Results may differ from a plain program's by a relative error of at most 0.014.
Values may be sent and summed in bfloat16 or wider, within the bound.
No kernel may reach another device: no remote copies, remote signals or barrier semaphores. Data moves between devices by JAX's collectives and lax.ppermute only.
A program may use at most 64 MiB of HBM per device.

v0:
```python
import jax
import jax.numpy as jnp
from jax import lax
from jax.sharding import PartitionSpec as P

EPS = 1e-06


def batched(matrix, vector):
    return jnp.einsum("suv,sv->su", matrix, vector, precision=lax.Precision.HIGHEST)


def shared(matrix, vector):
    return jnp.einsum("uv,sv->su", matrix, vector, precision=lax.Precision.HIGHEST)


def detector(gram_re, gram_im, match_re, match_im, steps, noise):
    sol_re = jnp.zeros_like(match_re)
    sol_im = jnp.zeros_like(match_im)
    resid_re, resid_im = (match_re, match_im)
    energy = jnp.sum(resid_re * resid_re + resid_im * resid_im, axis=1) + EPS
    earlier = energy
    prev_re, prev_im = (sol_re, sol_im)
    for index in range(steps.shape[0]):
        w_re, w_im = (steps[index, 0], steps[index, 1])
        dir_re = resid_re + shared(w_re, resid_re) - shared(w_im, resid_im)
        dir_im = resid_im + shared(w_re, resid_im) + shared(w_im, resid_re)
        if index > 0:
            ratio = (energy / earlier)[:, None]
            dir_re = dir_re + ratio * prev_re
            dir_im = dir_im + ratio * prev_im
        img_re = batched(gram_re, dir_re) - batched(gram_im, dir_im) + noise[:, None] * dir_re
        img_im = batched(gram_re, dir_im) + batched(gram_im, dir_re) + noise[:, None] * dir_im
        along = jnp.sum(dir_re * resid_re + dir_im * resid_im, axis=1)
        curvature = jnp.sum(dir_re * img_re + dir_im * img_im, axis=1) + EPS
        alpha = (along / curvature)[:, None]
        sol_re = sol_re + alpha * dir_re
        sol_im = sol_im + alpha * dir_im
        resid_re = resid_re - alpha * img_re
        resid_im = resid_im - alpha * img_im
        earlier = energy
        energy = jnp.sum(resid_re * resid_re + resid_im * resid_im, axis=1) + EPS
        prev_re, prev_im = (dir_re, dir_im)
    return (sol_re, sol_im)


def inner(form, left, right):
    return jnp.einsum(form, left, right, preferred_element_type=jnp.float32)


def partial_gram(chan, recv):
    h_re, h_im = (chan[0], chan[1])
    y_re, y_im = (recv[0], recv[1])
    gram_re = inner("sau,sav->suv", h_re, h_re) + inner("sau,sav->suv", h_im, h_im)
    gram_im = inner("sau,sav->suv", h_re, h_im) - inner("sau,sav->suv", h_im, h_re)
    match_re = inner("sau,sa->su", h_re, y_re) + inner("sau,sa->su", h_im, y_im)
    match_im = inner("sau,sa->su", h_re, y_im) - inner("sau,sa->su", h_im, y_re)
    return (gram_re, gram_im, match_re, match_im)


def adjoint(gram_re, gram_im, match_re, match_im, steps, noise_part, cot_re, cot_im):

    def forward(g_re, g_im, m_re, m_im, w_all):
        return detector(g_re, g_im, m_re, m_im, w_all, noise_part)

    outputs, pullback = jax.vjp(forward, gram_re, gram_im, match_re, match_im, steps)
    grads = pullback((cot_re, cot_im))
    sym = (grads[0] + jnp.swapaxes(grads[0], 1, 2)).astype(jnp.bfloat16)
    anti = (grads[1] - jnp.swapaxes(grads[1], 1, 2)).astype(jnp.bfloat16)
    return (sym, anti, grads[2].astype(jnp.bfloat16), grads[3].astype(jnp.bfloat16), grads[4])


def chain_rule(chan, recv, sym, anti, back_re, back_im):
    h_re, h_im = (chan[0], chan[1])
    yr32 = recv[0].astype(jnp.float32)
    yi32 = recv[1].astype(jnp.float32)
    br32 = back_re.astype(jnp.float32)
    bi32 = back_im.astype(jnp.float32)
    grad_hre = inner("sav,svu->sau", h_re, sym) - inner("sav,svu->sau", h_im, anti)
    grad_hre = grad_hre + yr32[:, :, None] * br32[:, None, :] + yi32[:, :, None] * bi32[:, None, :]
    grad_him = inner("sav,svu->sau", h_im, sym) + inner("sav,svu->sau", h_re, anti)
    grad_him = grad_him + yi32[:, :, None] * br32[:, None, :] - yr32[:, :, None] * bi32[:, None, :]
    grad_yre = inner("sau,su->sa", h_re, back_re) - inner("sau,su->sa", h_im, back_im)
    grad_yim = inner("sau,su->sa", h_im, back_re) + inner("sau,su->sa", h_re, back_im)
    grad_chan = jnp.stack([grad_hre, grad_him]).astype(jnp.bfloat16)
    grad_recv = jnp.stack([grad_yre, grad_yim]).astype(jnp.bfloat16)
    return (grad_chan, grad_recv)


def on_device(channel, received, noise, steps, cotangent, counts):
    panels = lax.axis_size("panel")
    width = channel.shape[1] // panels
    first = lax.axis_index("panel") * width
    cot_here = lax.all_to_all(cotangent, "panel", split_axis=1, concat_axis=2, tiled=True)
    position = first + jnp.arange(width, dtype=jnp.int32)
    live = (position < counts[0]).astype(jnp.float32)[:, None]
    cot_re = cot_here[0] * live
    cot_im = cot_here[1] * live
    noise_part = lax.dynamic_slice_in_dim(noise, first, width, 0)
    terms = partial_gram(channel, received)
    gram_re, gram_im, match_re, match_im = (
        lax.psum_scatter(
            terms[0].astype(jnp.bfloat16), "panel", scatter_dimension=0, tiled=True
        ).astype(jnp.float32),
        lax.psum_scatter(
            terms[1].astype(jnp.bfloat16), "panel", scatter_dimension=0, tiled=True
        ).astype(jnp.float32),
        lax.psum_scatter(
            terms[2].astype(jnp.bfloat16), "panel", scatter_dimension=0, tiled=True
        ).astype(jnp.float32),
        lax.psum_scatter(
            terms[3].astype(jnp.bfloat16), "panel", scatter_dimension=0, tiled=True
        ).astype(jnp.float32),
    )
    sym, anti, back_re, back_im, grad_w = adjoint(
        gram_re, gram_im, match_re, match_im, steps, noise_part, cot_re, cot_im
    )
    sym_all, anti_all, bre_all, bim_all = (
        lax.all_gather(sym, "panel", axis=0, tiled=True),
        lax.all_gather(anti, "panel", axis=0, tiled=True),
        lax.all_gather(back_re, "panel", axis=0, tiled=True),
        lax.all_gather(back_im, "panel", axis=0, tiled=True),
    )
    grad_channel, grad_received = chain_rule(channel, received, sym_all, anti_all, bre_all, bim_all)
    grad_steps = lax.psum(grad_w, ("panel", "sc"))
    return (grad_channel, grad_received, grad_steps)


def solution(mesh):
    return jax.shard_map(
        on_device,
        mesh=mesh,
        in_specs=(
            P(None, "sc", "panel", None),
            P(None, "sc", "panel"),
            P("sc"),
            P(),
            P(None, "sc", "panel"),
            P("sc"),
        ),
        out_specs=(P(None, "sc", "panel", None), P(None, "sc", "panel"), P()),
        check_vma=False,
    )
```

profile of v0, /device:TPU:1, one launch (start us, length us, event | category | flops | bytes accessed | tf_op | source)
XLA Modules:
  0.0 460.5 jit_solution(10206780318606603002)
XLA Ops:
  7.2 2.2 fusion.63
  9.4 1.5 add_convert_fusion
  11.8 10.0 %all-to-all-start = ((f32[8,1,128]{2,1,0:T(1,128)}), f32[8,1,128]{2,1,0:T(1,128)S(1)}, u32[]{:S(2)}, u32[]{:S(2)}) async-start(f32[8,1,128]{2,1,0:T(1,128)} %reshape.159), calls=%async_computation.2 | async-start | bytes 8192 | tf_op jit(solution)/shard_map/all_to_all | solution.py:94
  22.4 1.5 subtract_convert_fusion
  26.8 1.3 dynamic-slice
  28.7 22.9 %all-reduce.8 = (bf16[32,128]{1,0:T(8,128)(2,1)S(1)}, bf16[32,128]{1,0:T(8,128)(2,1)S(1)}) all-reduce(bf16[32,128]{1,0:T(8,128)(2,1)S(1)} %add_convert_fusion.2, bf16[32,128]{1,0:T(8,128)(2,1)S(1)} %subtract_convert_fusion.2), channel_id=3, replica_groups=mesh['panel'=8,'sc'=64] {'panel'}, use_global_device_ids=true, to_apply=%region_1.0.clone | all-reduce | flops 8192 | bytes 32768
  54.1 1.3 fusion.189
  55.3 1.2 fusion.191
  56.5 35.6 %reduce-scatter.5.cloned.1.call-done = bf16[4,128,128]{2,1,0:T(8,128)(2,1)} async-done(((bf16[32,128,128]{2,1,0:T(8,128)(2,1)}), bf16[4,128,128]{2,1,0:T(8,128)(2,1)}) %reduce-scatter.5.cloned.1.call-update) | async-done | bytes 131088 | tf_op jit(solution)/shard_map/reduce_scatter | solution.py:105
  92.2 1.3 fusion.190
  93.4 1.2 fusion.192
  96.0 1.2 fusion.194
  97.2 1.2 fusion.195
  98.4 1.2 fusion.193
  99.6 1.2 fusion.196
  102.2 1.2 fusion.200
  103.4 1.2 fusion.197
  104.6 1.2 fusion.199
  105.9 1.2 fusion.198
  114.3 1.9 fusion.69
  119.7 0.9 fusion.211
  123.2 9.9 %all-gather.1 = bf16[8,4,128]{2,1,0:T(4,128)(2,1)S(1)} all-gather(bf16[1,4,128]{2,1,0:T(4,128)(2,1)S(1)} %fusion.37), channel_id=1, replica_groups=mesh['panel'=8,'sc'=64] {'panel'}, dimensions={0}, use_global_device_ids=true | all-gather | bytes 9216 | tf_op jit(solution)/shard_map/all_gather | solution.py:122
  134.7 10.0 %all-gather = bf16[8,4,128]{2,1,0:T(4,128)(2,1)S(1)} all-gather(bf16[1,4,128]{2,1,0:T(4,128)(2,1)S(1)} %fusion.38), channel_id=1, replica_groups=mesh['panel'=8,'sc'=64] {'panel'}, dimensions={0}, use_global_device_ids=true | all-gather | bytes 9216 | tf_op jit(solution)/shard_map/all_gather | solution.py:121
  144.7 0.9 fusion.218
  153.7 3.5 fusion.43
  157.2 2.2 fusion.59
  159.5 17.7 %all-gather.7.cloned.1.call-done = bf16[32,128,128]{2,1,0:T(8,128)(2,1)} async-done(((bf16[4,128,128]{2,1,0:T(8,128)(2,1)}), bf16[32,128,128]{2,1,0:T(8,128)(2,1)}) %all-gather.7.cloned.1.call-update) | async-done | bytes 1048592 | tf_op jit(solution)/shard_map/all_gather | solution.py:120
  177.2 3.3 fusion.5
  180.4 1.7 fusion.4
  182.4 2.7 copy.41
  185.1 267.1 %all-reduce.11.cloned.1.call-done = f32[3,2,128,128]{3,2,1,0:T(8,128)} async-done(((f32[3,2,128,128]{3,2,1,0:T(8,128)}), f32[3,2,128,128]{3,2,1,0:T(8,128)}) %all-reduce.11.cloned.1.call-update) | async-done | bytes 393232 | tf_op jit(solution)/shard_map/psum | solution.py:125
  452.2 1.8 copy.119
  (228 shorter events, 31.0 us)
Async XLA Ops:
  7.2 46.9 %reduce-scatter.3.cloned.1.call-start = ((), (), s32[]{:S(2)}) async-start(), calls=%async_computation.3 | async-start | bytes 1179648 | tf_op jit(solution)/shard_map/reduce_scatter | solution.py:102
  11.8 40.7 %all-to-all-start = ((f32[8,1,128]{2,1,0:T(1,128)}), f32[8,1,128]{2,1,0:T(1,128)S(1)}, u32[]{:S(2)}, u32[]{:S(2)}) async-start(f32[8,1,128]{2,1,0:T(1,128)} %reshape.159), calls=%async_computation.2 | async-start | bytes 8192 | tf_op jit(solution)/shard_map/all_to_all | solution.py:94
  21.8 70.3 %reduce-scatter.5.cloned.1.call-start = ((), (), s32[]{:S(2)}) async-start(), calls=%async_computation.4 | async-start | bytes 1179648 | tf_op jit(solution)/shard_map/reduce_scatter | solution.py:105
  23.9 129.8 %all-gather.5.cloned.1.call-start = ((), (), s32[]{:S(2)}) async-start(), calls=%async_computation.5 | async-start | bytes 1179648 | tf_op jit(solution)/shard_map/all_gather | solution.py:119
  25.0 26.7 %copy-start.4 = (f32[3,2,128,128]{3,2,1,0:T(8,128)S(1)}, f32[3,2,128,128]{3,2,1,0:T(8,128)}, u32[]{:S(2)}) copy-start(f32[3,2,128,128]{3,2,1,0:T(8,128)} %param.9) | copy-start | bytes 1179652
  25.4 27.1 %copy-start.53 = (f32[32]{0:T(128)S(1)}, f32[32]{0:T(128)}, u32[]{:S(2)}) copy-start(f32[32]{0:T(128)} %param.8) | copy-start | bytes 388
  51.6 49.9 %copy-start.23 = (bf16[4,128]{1,0:T(4,128)(2,1)}, bf16[4,128]{1,0:T(4,128)(2,1)S(1)}, u32[]{:S(2)}) copy-start(bf16[4,128]{1,0:T(4,128)(2,1)S(1)} %get-tuple-element.87) | copy-start | bytes 3076
  51.7 50.1 %copy-start.25 = (bf16[4,128]{1,0:T(4,128)(2,1)}, bf16[4,128]{1,0:T(4,128)(2,1)S(1)}, u32[]{:S(2)}) copy-start(bf16[4,128]{1,0:T(4,128)(2,1)S(1)} %get-tuple-element.86) | copy-start | bytes 3076
  52.4 58.7 %copy-start.45 = (f32[4]{0:T(128)}, f32[4]{0:T(128)S(1)}, u32[]{:S(2)}) copy-start(f32[4]{0:T(128)S(1)} %compare_convert_fusion) | copy-start | bytes 52
  52.5 58.5 %copy-start.38 = (f32[4]{0:T(128)}, f32[4]{0:T(128)S(1)}, u32[]{:S(2)}) copy-start(f32[4]{0:T(128)S(1)} %dynamic_slice.3) | copy-start | bytes 52
  53.9 58.3 %copy-start.36 = (f32[4,128]{1,0:T(4,128)}, f32[4,128]{1,0:T(4,128)S(1)}, u32[]{:S(2)}) copy-start(f32[4,128]{1,0:T(4,128)S(1)} %squeeze.55) | copy-start | bytes 6148
  54.0 58.5 %copy-start.37 = (f32[4,128]{1,0:T(4,128)}, f32[4,128]{1,0:T(4,128)S(1)}, u32[]{:S(2)}) copy-start(f32[4,128]{1,0:T(4,128)S(1)} %squeeze.53) | copy-start | bytes 6148
  54.0 53.4 %copy-start.1 = (bf16[4,128,128]{2,1,0:T(8,128)(2,1)S(1)}, bf16[4,128,128]{2,1,0:T(8,128)(2,1)}, u32[]{:S(2)}) copy-start(bf16[4,128,128]{2,1,0:T(8,128)(2,1)} %reduce-scatter.3.cloned.1.call-done) | copy-start | bytes 393220
  92.2 15.5 %copy-start.2 = (bf16[4,128,128]{2,1,0:T(8,128)(2,1)S(1)}, bf16[4,128,128]{2,1,0:T(8,128)(2,1)}, u32[]{:S(2)}) copy-start(bf16[4,128,128]{2,1,0:T(8,128)(2,1)} %reduce-scatter.5.cloned.1.call-done) | copy-start | bytes 393220
  94.9 18.9 %copy-start.43 = (f32[4,128]{1,0:T(4,128)}, f32[4,128]{1,0:T(4,128)S(1)}, u32[]{:S(2)}) copy-start(f32[4,128]{1,0:T(4,128)S(1)} %get-tuple-element.56) | copy-start | bytes 6148
  94.9 18.9 %copy-start.44 = (f32[4,128]{1,0:T(4,128)}, f32[4,128]{1,0:T(4,128)S(1)}, u32[]{:S(2)}) copy-start(f32[4,128]{1,0:T(4,128)S(1)} %get-tuple-element.57) | copy-start | bytes 6148
  94.9 18.9 %copy-start.51 = (f32[4]{0:T(128)}, f32[4]{0:T(128)S(1)}, u32[]{:S(2)}) copy-start(f32[4]{0:T(128)S(1)} %fusion.179) | copy-start | bytes 52
  95.1 18.7 %copy-start.9 = (f32[4,128]{1,0:T(4,128)}, f32[4,128]{1,0:T(4,128)S(1)}, u32[]{:S(2)}) copy-start(f32[4,128]{1,0:T(4,128)S(1)} %get-tuple-element.55) | copy-start | bytes 6148
  95.1 18.7 %copy-start.11 = (f32[4,128]{1,0:T(4,128)}, f32[4,128]{1,0:T(4,128)S(1)}, u32[]{:S(2)}) copy-start(f32[4,128]{1,0:T(4,128)S(1)} %get-tuple-element.54) | copy-start | bytes 6148
  95.5 6.7 %copy-start.50 = (f32[4]{0:T(128)}, f32[4]{0:T(128)S(1)}, u32[]{:S(2)}) copy-start(f32[4]{0:T(128)S(1)} %fusion.180) | copy-start | bytes 52
  101.3 12.5 %copy-start.15 = (f32[4,128]{1,0:T(4,128)}, f32[4,128]{1,0:T(4,128)S(1)}, u32[]{:S(2)}) copy-start(f32[4,128]{1,0:T(4,128)S(1)} %get-tuple-element.49) | copy-start | bytes 6148
  101.3 12.5 %copy-start.17 = (f32[4,128]{1,0:T(4,128)}, f32[4,128]{1,0:T(4,128)S(1)}, u32[]{:S(2)}) copy-start(f32[4,128]{1,0:T(4,128)S(1)} %get-tuple-element.50) | copy-start | bytes 6148
  101.9 11.9 %copy-start.7 = (f32[4,128]{1,0:T(4,128)}, f32[4,128]{1,0:T(4,128)S(1)}, u32[]{:S(2)}) copy-start(f32[4,128]{1,0:T(4,128)S(1)} %fusion.19) | copy-start | bytes 6148
  102.2 11.7 %copy-start.8 = (f32[4,128]{1,0:T(4,128)}, f32[4,128]{1,0:T(4,128)S(1)}, u32[]{:S(2)}) copy-start(f32[4,128]{1,0:T(4,128)S(1)} %fusion.17) | copy-start | bytes 6148
  107.5 6.4 %copy-start.33 = (f32[4,128]{1,0:T(4,128)}, f32[4,128]{1,0:T(4,128)S(1)}, u32[]{:S(2)}) copy-start(f32[4,128]{1,0:T(4,128)S(1)} %get-tuple-element.77) | copy-start | bytes 6148
  107.5 6.4 %copy-start.39 = (f32[4,128]{1,0:T(4,128)}, f32[4,128]{1,0:T(4,128)S(1)}, u32[]{:S(2)}) copy-start(f32[4,128]{1,0:T(4,128)S(1)} %get-tuple-element.76) | copy-start | bytes 6148
  108.1 5.8 %copy-start.19 = (f32[4,128]{1,0:T(4,128)}, f32[4,128]{1,0:T(4,128)S(1)}, u32[]{:S(2)}) copy-start(f32[4,128]{1,0:T(4,128)S(1)} %get-tuple-element.45) | copy-start | bytes 6148
  108.1 5.8 %copy-start.40 = (f32[4,128]{1,0:T(4,128)}, f32[4,128]{1,0:T(4,128)S(1)}, u32[]{:S(2)}) copy-start(f32[4,128]{1,0:T(4,128)S(1)} %get-tuple-element.68) | copy-start | bytes 6148
  116.2 60.9 %all-gather.7.cloned.1.call-start = ((), (), s32[]{:S(2)}) async-start(), calls=%async_computation.6 | async-start | bytes 1179648 | tf_op jit(solution)/shard_map/all_gather | solution.py:120
  149.2 303.0 %all-reduce.11.cloned.1.call-start = ((), (), s32[]{:S(2)}) async-start(), calls=%async_computation.7 | async-start | bytes 786432 | tf_op jit(solution)/shard_map/psum | solution.py:125
  157.2 19.9 %copy-start.13 = (f32[32,128]{1,0:T(8,128)S(1)}, f32[32,128]{1,0:T(8,128)}, u32[]{:S(2)}) copy-start(f32[32,128]{1,0:T(8,128)} %get-tuple-element.64) | copy-start | bytes 49156
  157.2 19.9 %copy-start.14 = (f32[32,128]{1,0:T(8,128)S(1)}, f32[32,128]{1,0:T(8,128)}, u32[]{:S(2)}) copy-start(f32[32,128]{1,0:T(8,128)} %get-tuple-element.67) | copy-start | bytes 49156
  (28 other events, 80.9 us)
Sparse Core Ops, SparseCore 0:
  11.4 41.5 reduce-scatter.2
  55.8 36.3 reduce-scatter.4
  116.3 29.5 all-gather.4
  149.3 27.7 all-gather.6
  182.6 269.5 all-reduce.10
where the time goes:
time: 461 us; the launch traced here: 460 us
  waiting for transfers between devices  321 us (70%)
  matrix products  52.6 us (11%)
  blocking collectives  42.8 us (9%)
  between operations  16.1 us (3%)
  other arithmetic  10.3 us (2%)
  starting transfers between devices  10.2 us (2%)
  local copies, waits for them, and re-layouts  8.03 us (2%)
    psum x1, waiting for transfers between devices, on_device(): grad_steps = lax.psum(grad_w, ('panel', 'sc'))  267 us
    reduce_scatter x1, waiting for transfers between devices, on_device(): lax.psum_scatter(terms[1].astype(jnp.bfloat16), 'panel', scatter_dimensio...  35.6 us
    unnamed x1, blocking collectives  22.9 us
    dot_general x16, matrix products, inner(): return jnp.einsum(form, left, right, preferred_element_type=jnp.float32)  20.6 us
    dot_general x24, matrix products, batched(): jnp.einsum('suv,sv->su', matrix, vector, precision=lax.Precision.HIGHEST)  20 us
    all_gather x1, waiting for transfers between devices, on_device(): lax.all_gather(anti, 'panel', axis=0, tiled=True)  17.7 us
    dot_general x36, matrix products, shared(): jnp.einsum('uv,sv->su', matrix, vector, precision=lax.Precision.HIGHEST)  12 us
    all_to_all x1, starting transfers between devices, on_device(): lax.all_to_all(cotangent, 'panel', split_axis=1, concat_axis=2, tiled=True)  10 us
  transfers between devices with their start and end apart: 6, of which 3 were waited for; matrix products, arithmetic and copies ran while one was open for 9% of the time, Pallas kernels for 0%

commit v1 on v0

--- a/solution.py
+++ b/solution.py
@@ -4,6 +4,28 @@
 from jax.sharding import PartitionSpec as P
 
 EPS = 1e-06
+
+
+def laid_out(blocks, dim):
+    dims = list(blocks.shape[1:])
+    dims[dim] *= blocks.shape[0]
+    return jnp.moveaxis(blocks, 0, dim).reshape(dims)
+
+
+def collect(x, axis, dim):
+    size = lax.axis_size(axis)
+    pairs = [(i, (i + 1) % size) for i in range(size)]
+    back = [(b, a) for a, b in pairs]
+    lower, upper = ([], [])
+    for step in range(size - 1):
+        if step % 2 == 0:
+            lower.append(lax.ppermute(lower[-1] if lower else x, axis, pairs))
+        else:
+            upper.append(lax.ppermute(upper[-1] if upper else x, axis, back))
+    blocks = jnp.stack([*lower[::-1], x, *upper])
+    shift = lax.axis_index(axis) - len(lower)
+    blocks = blocks[(jnp.arange(size) - shift) % size]
+    return laid_out(blocks, dim)
 
 
 def batched(matrix, vector):
@@ -117,7 +139,7 @@
     )
     sym_all, anti_all, bre_all, bim_all = (
         lax.all_gather(sym, "panel", axis=0, tiled=True),
-        lax.all_gather(anti, "panel", axis=0, tiled=True),
+        collect(anti, "panel", 0),
         lax.all_gather(back_re, "panel", axis=0, tiled=True),
         lax.all_gather(back_im, "panel", axis=0, tiled=True),
     )

time: 461 us -> 453 us (0.983)
  starting transfers between devices: 10.2 us -> 22.2 us
  waiting for transfers between devices: 321 us -> 309 us
  matrix products: 52.6 us -> 40.9 us
  local copies, waits for them, and re-layouts: 8.03 us -> 15.1 us
    all_gather x1 -> x0, waiting for transfers between devices: 17.7 us -> none  [on_device(): lax.all_gather(anti, 'panel', axis=0, tiled=True)]
    ppermute x0 -> x7, starting transfers between devices: none -> 11.9 us  [the longest x4 8.79 us: collect(): lower.append(lax.ppermute(lower[-1] if lower else x, axis, pairs))]
    all_gather x1, waiting for transfers between devices: 0.02 us -> 4.96 us  [on_device(): lax.all_gather(sym, 'panel', axis=0, tiled=True)]
    unnamed x115 -> x30, local copies, waits for them, and re-layouts: 7.01 us -> 11.4 us
  transfers between devices with their start and end apart: 6 -> 12, of which waited for: 3 -> 5; matrix products, arithmetic and copies ran while one was open for 9% -> 7% of each run, Pallas kernels for 0% -> 0%
where the time goes in v1:
time: 453 us; the launch traced here: 452 us
  waiting for transfers between devices  309 us (68%)
  blocking collectives  42.7 us (9%)
  matrix products  40.9 us (9%)
  starting transfers between devices  22.2 us (5%)
  between operations  15.6 us (3%)
  local copies, waits for them, and re-layouts  15.1 us (3%)
  other arithmetic  6.32 us (1%)
    psum x1, waiting for transfers between devices, on_device(): grad_steps = lax.psum(grad_w, ('panel', 'sc'))  266 us
    reduce_scatter x1, waiting for transfers between devices, on_device(): lax.psum_scatter(terms[1].astype(jnp.bfloat16), 'panel', scatter_dimensio...  36.2 us
    unnamed x1, blocking collectives  22.9 us
    dot_general x24, matrix products, batched(): jnp.einsum('suv,sv->su', matrix, vector, precision=lax.Precision.HIGHEST)  16.5 us
    dot_general x16, matrix products, inner(): return jnp.einsum(form, left, right, preferred_element_type=jnp.float32)  16.3 us
    unnamed x30, local copies, waits for them, and re-layouts  11.4 us
    all_to_all x1, starting transfers between devices, on_device(): lax.all_to_all(cotangent, 'panel', split_axis=1, concat_axis=2, tiled=True)  10 us
    all_gather x1, blocking collectives, on_device(): lax.all_gather(back_im, 'panel', axis=0, tiled=True)  9.91 us
  transfers between devices with their start and end apart: 12, of which 5 were waited for; matrix products, arithmetic and copies ran while one was open for 7% of the time, Pallas kernels for 0%

profile of v1, /device:TPU:1, one launch (start us, length us, event | category | flops | bytes accessed | tf_op | source)
XLA Modules:
  0.0 452.1 jit_solution(17508940575917114004)
XLA Ops:
  7.2 2.2 fusion.63
  9.4 1.5 add_convert_fusion
  11.8 10.0 %all-to-all-start = ((f32[8,1,128]{2,1,0:T(1,128)}), f32[8,1,128]{2,1,0:T(1,128)S(1)}, u32[]{:S(2)}, u32[]{:S(2)}) async-start(f32[8,1,128]{2,1,0:T(1,128)} %reshape.220), calls=%async_computation.2 | async-start | bytes 8192 | tf_op jit(solution)/shard_map/all_to_all | solution.py:116
  22.4 1.5 subtract_convert_fusion
  26.2 1.3 dynamic-slice
  28.2 22.9 %all-reduce.8 = (bf16[32,128]{1,0:T(8,128)(2,1)S(1)}, bf16[32,128]{1,0:T(8,128)(2,1)S(1)}) all-reduce(bf16[32,128]{1,0:T(8,128)(2,1)S(1)} %add_convert_fusion.2, bf16[32,128]{1,0:T(8,128)(2,1)S(1)} %subtract_convert_fusion.2), channel_id=3, replica_groups=mesh['panel'=8,'sc'=64] {'panel'}, use_global_device_ids=true, to_apply=%region_1.0.clone | all-reduce | flops 8192 | bytes 32768
  53.5 1.3 fusion.193
  54.8 1.2 fusion.191
  56.0 36.2 %reduce-scatter.5.cloned.1.call-done = bf16[4,128,128]{2,1,0:T(8,128)(2,1)} async-done(((bf16[32,128,128]{2,1,0:T(8,128)(2,1)}), bf16[4,128,128]{2,1,0:T(8,128)(2,1)}) %reduce-scatter.5.cloned.1.call-update) | async-done | bytes 131088 | tf_op jit(solution)/shard_map/reduce_scatter | solution.py:127
  92.2 1.3 fusion.194
  93.5 1.2 fusion.192
  96.0 1.2 fusion.197
  98.4 1.2 fusion.198
  99.6 1.2 fusion.195
  102.1 1.2 fusion.201
  103.4 1.2 fusion.200
  112.7 9.9 %all-gather.1 = bf16[8,4,128]{2,1,0:T(4,128)(2,1)S(1)} all-gather(bf16[1,4,128]{2,1,0:T(4,128)(2,1)S(1)} %fusion.37), channel_id=1, replica_groups=mesh['panel'=8,'sc'=64] {'panel'}, dimensions={0}, use_global_device_ids=true | all-gather | bytes 9216 | tf_op jit(solution)/shard_map/all_gather | solution.py:144
  124.1 9.8 %all-gather = bf16[8,4,128]{2,1,0:T(4,128)(2,1)S(1)} all-gather(bf16[1,4,128]{2,1,0:T(4,128)(2,1)S(1)} %fusion.38), channel_id=1, replica_groups=mesh['panel'=8,'sc'=64] {'panel'}, dimensions={0}, use_global_device_ids=true | all-gather | bytes 9216 | tf_op jit(solution)/shard_map/all_gather | solution.py:143
  137.8 1.6 collective-permute-start
  141.4 2.3 collective-permute-start.1
  144.3 1.4 collective-permute-done.1
  145.7 2.4 collective-permute-start.2
  150.1 2.4 collective-permute-start.3
  153.9 2.1 collective-permute-start.6
  161.3 2.0 gather_fusion
  163.3 5.0 %all-gather.4.cloned.1.call-done = bf16[32,128,128]{2,1,0:T(8,128)(2,1)} async-done(((bf16[4,128,128]{2,1,0:T(8,128)(2,1)}), bf16[32,128,128]{2,1,0:T(8,128)(2,1)}) %all-gather.4.cloned.1.call-update) | async-done | bytes 1048592 | tf_op jit(solution)/shard_map/all_gather | solution.py:141
  168.3 2.1 fusion.43
  170.4 1.7 fusion.5
  173.0 1.7 fusion.4
  174.9 2.7 copy.41
  177.6 266.2 %all-reduce.11.cloned.1.call-done = f32[3,2,128,128]{3,2,1,0:T(8,128)} async-done(((f32[3,2,128,128]{3,2,1,0:T(8,128)}), f32[3,2,128,128]{3,2,1,0:T(8,128)}) %all-reduce.11.cloned.1.call-update) | async-done | bytes 393232 | tf_op jit(solution)/shard_map/psum | solution.py:147
  443.8 1.8 copy.126
  (158 shorter events, 34.6 us)
Async XLA Ops:
  7.2 2.3 copy-start
  7.2 46.3 %reduce-scatter.3.cloned.1.call-start = ((), (), s32[]{:S(2)}) async-start(), calls=%async_computation.3 | async-start | bytes 1179648 | tf_op jit(solution)/shard_map/reduce_scatter | solution.py:124
  9.4 1.6 copy-start.5
  11.8 40.2 %all-to-all-start = ((f32[8,1,128]{2,1,0:T(1,128)}), f32[8,1,128]{2,1,0:T(1,128)S(1)}, u32[]{:S(2)}, u32[]{:S(2)}) async-start(f32[8,1,128]{2,1,0:T(1,128)} %reshape.220), calls=%async_computation.2 | async-start | bytes 8192 | tf_op jit(solution)/shard_map/all_to_all | solution.py:116
  21.8 70.4 %reduce-scatter.5.cloned.1.call-start = ((), (), s32[]{:S(2)}) async-start(), calls=%async_computation.4 | async-start | bytes 1179648 | tf_op jit(solution)/shard_map/reduce_scatter | solution.py:127
  22.4 1.6 copy-start.6
  23.9 144.4 %all-gather.4.cloned.1.call-start = ((), (), s32[]{:S(2)}) async-start(), calls=%async_computation.5 | async-start | bytes 1179648 | tf_op jit(solution)/shard_map/all_gather | solution.py:141
  24.4 26.8 %copy-start.3 = (f32[3,2,128,128]{3,2,1,0:T(8,128)S(1)}, f32[3,2,128,128]{3,2,1,0:T(8,128)}, u32[]{:S(2)}) copy-start(f32[3,2,128,128]{3,2,1,0:T(8,128)} %param.9) | copy-start | bytes 1179652
  24.8 27.1 %copy-start.7 = (f32[32]{0:T(128)S(1)}, f32[32]{0:T(128)}, u32[]{:S(2)}) copy-start(f32[32]{0:T(128)} %param.8) | copy-start | bytes 388
  53.5 52.3 %copy-start.1 = (bf16[4,128,128]{2,1,0:T(8,128)(2,1)S(1)}, bf16[4,128,128]{2,1,0:T(8,128)(2,1)}, u32[]{:S(2)}) copy-start(bf16[4,128,128]{2,1,0:T(8,128)(2,1)} %reduce-scatter.3.cloned.1.call-done) | copy-start | bytes 393220
  92.2 14.6 %copy-start.2 = (bf16[4,128,128]{2,1,0:T(8,128)(2,1)S(1)}, bf16[4,128,128]{2,1,0:T(8,128)(2,1)}, u32[]{:S(2)}) copy-start(bf16[4,128,128]{2,1,0:T(8,128)(2,1)} %reduce-scatter.5.cloned.1.call-done) | copy-start | bytes 393220
  137.6 11.1 %collective-permute-start.4 = (bf16[4,128,128]{2,1,0:T(8,128)(2,1)S(1)}, bf16[4,128,128]{2,1,0:T(8,128)(2,1)S(1)}, u32[]{:S(2)}, u32[]{:S(2)}) collective-permute-start(bf16[4,128,128]{2,1,0:T(8,128)(2,1)S(1)} %get-tuple-element.60), channel_id=1, source_target_pairs={{64,0},{128,64},{192,128},{256,192},{320,256},{384,320},{448,384},... | collective-permute-start | bytes 393224 | tf_op jit(solution)/shard_map/ppermute | solution.py:24
  137.8 3.6 collective-permute-start
  139.4 304.4 %all-reduce.11.cloned.1.call-start = ((), (), s32[]{:S(2)}) async-start(), calls=%async_computation.6 | async-start | bytes 786432 | tf_op jit(solution)/shard_map/psum | solution.py:147
  141.4 4.3 collective-permute-start.1
  145.7 4.4 collective-permute-start.2
  148.7 5.2 %collective-permute-start.5 = (bf16[4,128,128]{2,1,0:T(8,128)(2,1)S(1)}, bf16[4,128,128]{2,1,0:T(8,128)(2,1)S(1)}, u32[]{:S(2)}, u32[]{:S(2)}) collective-permute-start(bf16[4,128,128]{2,1,0:T(8,128)(2,1)S(1)} %collective-permute-done.4), channel_id=1, source_target_pairs={{64,0},{128,64},{192,128},{256,192},{320,256},{384,320},{448,384},... | collective-permute-start | bytes 393224 | tf_op jit(solution)/shard_map/ppermute | solution.py:24
  150.1 5.9 %collective-permute-start.3 = (bf16[4,128,128]{2,1,0:T(8,128)(2,1)S(1)}, bf16[4,128,128]{2,1,0:T(8,128)(2,1)S(1)}, u32[]{:S(2)}, u32[]{:S(2)}) collective-permute-start(bf16[4,128,128]{2,1,0:T(8,128)(2,1)S(1)} %collective-permute-done.2), channel_id=1, source_target_pairs={{0,64},{64,128},{128,192},{192,256},{256,320},{320,384},{384,448},... | collective-permute-start | bytes 393224 | tf_op jit(solution)/shard_map/ppermute | solution.py:22
  153.9 6.7 %collective-permute-start.6 = (bf16[4,128,128]{2,1,0:T(8,128)(2,1)S(1)}, bf16[4,128,128]{2,1,0:T(8,128)(2,1)S(1)}, u32[]{:S(2)}, u32[]{:S(2)}) collective-permute-start(bf16[4,128,128]{2,1,0:T(8,128)(2,1)S(1)} %collective-permute-done.5), channel_id=1, source_target_pairs={{64,0},{128,64},{192,128},{256,192},{320,256},{384,320},{448,384},... | collective-permute-start | bytes 393224 | tf_op jit(solution)/shard_map/ppermute | solution.py:24
  170.4 1.7 copy-start.4
Sparse Core Ops, SparseCore 0:
  11.4 41.5 reduce-scatter.2
  55.8 36.3 reduce-scatter.4
  139.5 28.7 all-gather.3
  173.7 270.0 all-reduce.10
